TPU v7x, 32 devices: a whole 2x2x4 slice. The times are simulated.
32 devices in a mesh: clips: 2 (over y), ha: 4 (over z), ta: 2 (over x), wa: 2 (over core).
Axes of the slice: x: 2, y: 2, z: 4, core: 2. Of those that a mesh axis runs over, the one named last changes fastest.
Arguments:
- frames: bfloat16 [8, 16, 128, 192], P(('clips', 'ta'), 'ha', 'wa'), parts along dimension 0, may hold values from -6 to 6
- cache: bfloat16 [4, 16, 128, 192], P('clips', 'ha', 'wa'), parts along dimension 0, may hold values from -5 to 5
- norm_gain: float32 [192], replicated, may hold values from 0.25 to 1.75
- conv_weight: bfloat16 [3, 3, 3, 192, 192], replicated, may hold values from -0.078125 to 0.078125
- conv_bias: float32 [192], replicated, may hold values from -3 to 3
- up_weight: bfloat16 [3, 3, 192, 96], replicated, may hold values from -0.15625 to 0.15625
- up_bias: float32 [96], replicated, may hold values from -3 to 3
Outputs:
- upsampled: bfloat16 [8, 32, 128, 192], P(('clips', 'ta'), 'ha', 'wa'), parts along dimension 0
There are 2 independent parts, one for each index of `clips`. A program takes and returns all parts, laid end to end along the dimension named above; an argument that names none is the same for every part. Nothing has to cross between parts.
All inputs are finite; a program needn't handle non-finite values.
Results may differ from a plain program's by a relative error of at most 0.0075.
Values may be sent and summed in bfloat16 or wider, within the bound.
A program may use at most 64 MiB of HBM per device.

v0:
```python
import jax
import jax.numpy as jnp
from jax import lax
from jax.sharding import PartitionSpec as P

EPS = 1e-06
PHASE_TAPS = (((0, (0,)), (1, (1, 2))), ((1, (0, 1)), (2, (2,))))


def shifted(shard, axis, by):
    devices = lax.axis_size(axis)
    pairs = [(i, i + by) for i in range(devices) if 0 <= i + by < devices]
    return lax.ppermute(shard, axis, pairs)


def padded_2(cells, sides, width):
    for axis, dim in sides:
        count = lax.axis_size(axis)
        ends = count - 1
        head = lax.slice_in_dim(cells, 0, width, axis=dim)
        tail = lax.slice_in_dim(cells, cells.shape[dim] - width, cells.shape[dim], axis=dim)
        cells = jnp.concatenate(
            [
                lax.ppermute(tail, axis, [(i, (i + 1) % count) for i in range(ends)]),
                cells,
                lax.ppermute(head, axis, [((i + 1) % count, i) for i in range(ends)]),
            ],
            axis=dim,
        )
    return cells


def activate(values, gain):
    wide = values.astype(jnp.float32)
    scale = lax.rsqrt(jnp.mean(wide * wide, axis=-1, keepdims=True) + EPS)
    return jax.nn.silu(wide * scale * gain).astype(jnp.bfloat16)


def causal_conv(padded, weight, count, rows, cols):
    channels = padded.shape[-1]
    total = jnp.zeros((count * rows * cols, weight.shape[-1]), jnp.float32)
    for a in range(3):
        for b in range(3):
            for c in range(3):
                window = padded[a : a + count, b : b + rows, c : c + cols].reshape(-1, channels)
                total = total + jnp.dot(window, weight[a, b, c], preferred_element_type=jnp.float32)
    return total.reshape(count, rows, cols, -1)


def upsample_conv(bordered, weight, bias):
    count = bordered.shape[0]
    rows = bordered.shape[1] - 2
    cols = bordered.shape[2] - 2
    channels = bordered.shape[-1]
    outputs = weight.shape[-1]
    row_phases = []
    for row_phase in range(2):
        col_phases = []
        for col_phase in range(2):
            total = jnp.zeros((count * rows * cols, outputs), jnp.float32)
            for row_start, row_taps in PHASE_TAPS[row_phase]:
                for col_start, col_taps in PHASE_TAPS[col_phase]:
                    window = bordered[
                        :, row_start : row_start + rows, col_start : col_start + cols
                    ].reshape(-1, channels)
                    if len(row_taps) * len(col_taps) == 1:
                        total = total + jnp.dot(
                            window,
                            weight[row_taps[0], col_taps[0]],
                            preferred_element_type=jnp.float32,
                        )
                    else:
                        folded = jnp.zeros((channels, outputs), jnp.float32)
                        for a in row_taps:
                            for b in col_taps:
                                folded = folded + weight[a, b].astype(jnp.float32)
                        upper = folded.astype(jnp.bfloat16)
                        lower = (folded - upper.astype(jnp.float32)).astype(jnp.bfloat16)
                        total = total + jnp.dot(window, upper, preferred_element_type=jnp.float32)
                        total = total + jnp.dot(window, lower, preferred_element_type=jnp.float32)
            result = (total + bias).astype(jnp.bfloat16)
            col_phases.append(result.reshape(count, rows, cols, outputs))
        row_phases.append(jnp.concatenate(col_phases, axis=-1))
    stacked = jnp.stack(row_phases, axis=2)
    return stacked.reshape(count, 2 * rows, cols, 2 * outputs)


def on_device(frames, cache, norm_gain, conv_weight, conv_bias, up_weight, up_bias):
    count, rows, cols, channels = frames.shape
    activated = activate(frames, norm_gain)
    earlier = shifted(activated, "ta", 1)
    earlier = jnp.where(lax.axis_index("ta") == 0, cache, earlier)
    extended = jnp.concatenate([earlier, activated], axis=0)
    padded = padded_2(extended, (("ha", 1), ("wa", 2)), 1)
    convolved = causal_conv(padded, conv_weight, count, rows, cols)
    residual = (frames.astype(jnp.float32) + convolved + conv_bias).astype(jnp.bfloat16)
    bordered = padded_2(residual, (("ha", 1), ("wa", 2)), 1)
    return upsample_conv(bordered, up_weight, up_bias)


def solution(mesh):
    return jax.shard_map(
        on_device,
        mesh=mesh,
        in_specs=(
            P(("clips", "ta"), "ha", "wa", None),
            P("clips", "ha", "wa", None),
            P(),
            P(),
            P(),
            P(),
            P(),
        ),
        out_specs=P(("clips", "ta"), "ha", "wa", None),
        check_vma=False,
    )
```

profile of v0, /device:TPU:0, one launch (start us, length us, event | category | flops | bytes accessed | tf_op | source)
XLA Modules:
  0.0 61.0 jit_solution(4402095644396140259)
XLA Ops:
  0.0 1.1 %fusion.14 = f32[2,4,64]{2,1,0:T(4,128)S(1)} fusion(bf16[2,4,64,192]{3,2,1,0:T(8,128)(2,1)} %param.7), kind=kLoop, calls=%fused_computation.65 | loop fusion | flops 294400 | bytes 198656 | tf_op jit(solution)/shard_map/reduce_sum | solution.py:35
  1.1 1.2 %fusion.21 = bf16[2,4,64,192]{3,2,1,0:T(8,128)(2,1)S(1)} fusion(bf16[2,4,64,192]{3,2,1,0:T(8,128)(2,1)} %param.7, f32[192]{0:T(256)} %param.9, f32[2,4,64]{2,1,0:T(4,128)S(1)} %add_rsqrt_fusion), kind=kLoop, calls=%fused_computation.72 | loop fusion | flops 786432 | bytes 396032 | tf_op jit(solution)/shard_map/convert_element_type | solution.py:36
  2.3 4.9 %collective-permute-start = (bf16[2,4,64,192]{3,2,1,0:T(8,128)(2,1)S(1)}, bf16[2,4,64,192]{3,2,1,0:T(8,128)(2,1)S(1)}, u32[]{:S(2)}, u32[]{:S(2)}) collective-permute-start(bf16[2,4,64,192]{3,2,1,0:T(8,128)(2,1)S(1)} %fusion.21), channel_id=1, source_target_pairs={{0,2},{1,3},{4,6},{5,7},{8,10},{9,11},{12,14},{13,15},{16,18},{17,... | collective-permute-start | bytes 589832 | tf_op jit(solution)/shard_map/ppermute | solution.py:13
  7.2 5.5 %collective-permute-done = bf16[2,4,64,192]{3,2,1,0:T(8,128)(2,1)S(1)} collective-permute-done((bf16[2,4,64,192]{3,2,1,0:T(8,128)(2,1)S(1)}, bf16[2,4,64,192]{3,2,1,0:T(8,128)(2,1)S(1)}, u32[]{:S(2)}, u32[]{:S(2)}) %collective-permute-start) | collective-permute-done | bytes 196640 | tf_op jit(solution)/shard_map/ppermute | solution.py:13
  12.7 1.0 %broadcast_select_fusion = bf16[2,4,64,192]{3,2,1,0:T(8,128)(2,1)S(1)} fusion(bf16[2,4,64,192]{3,2,1,0:T(8,128)(2,1)} %param.8, bf16[2,4,64,192]{3,2,1,0:T(8,128)(2,1)S(1)} %collective-permute-done, pred[]{:T(512)S(6)} %eq.3), kind=kLoop, calls=%fused_computation.83 | loop fusion | flops 98304 | bytes 589825 | tf_op jit(solution)/shard_map/jit(_where)/select_n | solution.py:92
  13.8 3.5 %collective-permute-start.1 = (bf16[4,1,64,192]{3,2,1,0:T(8,128)(2,1)S(1)}, bf16[4,1,64,192]{3,2,1,0:T(8,128)(2,1)S(1)}, u32[]{:S(2)}, u32[]{:S(2)}) collective-permute-start(bf16[4,1,64,192]{3,2,1,0:T(8,128)(2,1)S(1)} %get-tuple-element.35), channel_id=1, source_target_pairs={{0,4},{4,8},{8,12},{1,5},{5,9},{9,13},{2,6},{6,10},{10,14},{3,7},{... | collective-permute-start | bytes 294920 | tf_op jit(solution)/shard_map/ppermute | solution.py:24
  17.3 1.3 %collective-permute-start.2 = (bf16[4,1,64,192]{3,2,1,0:T(8,128)(2,1)S(1)}, bf16[4,1,64,192]{3,2,1,0:T(8,128)(2,1)S(1)}, u32[]{:S(2)}, u32[]{:S(2)}) collective-permute-start(bf16[4,1,64,192]{3,2,1,0:T(8,128)(2,1)S(1)} %get-tuple-element.36), channel_id=1, source_target_pairs={{4,0},{8,4},{12,8},{5,1},{9,5},{13,9},{6,2},{10,6},{14,10},{7,3},{... | collective-permute-start | bytes 294920 | tf_op jit(solution)/shard_map/ppermute | solution.py:26
  18.6 1.1 %collective-permute-done.1 = bf16[4,1,64,192]{3,2,1,0:T(8,128)(2,1)S(1)} collective-permute-done((bf16[4,1,64,192]{3,2,1,0:T(8,128)(2,1)S(1)}, bf16[4,1,64,192]{3,2,1,0:T(8,128)(2,1)S(1)}, u32[]{:S(2)}, u32[]{:S(2)}) %collective-permute-start.1) | collective-permute-done | bytes 98336 | tf_op jit(solution)/shard_map/ppermute | solution.py:24
  19.8 4.4 %collective-permute-done.2 = bf16[4,1,64,192]{3,2,1,0:T(8,128)(2,1)S(1)} collective-permute-done((bf16[4,1,64,192]{3,2,1,0:T(8,128)(2,1)S(1)}, bf16[4,1,64,192]{3,2,1,0:T(8,128)(2,1)S(1)}, u32[]{:S(2)}, u32[]{:S(2)}) %collective-permute-start.2) | collective-permute-done | bytes 98336 | tf_op jit(solution)/shard_map/ppermute | solution.py:26
  24.2 1.6 %collective-permute-start.3 = (bf16[4,6,1,192]{3,2,1,0:T(2,128)(2,1)S(1)}, bf16[4,6,1,192]{3,2,1,0:T(2,128)(2,1)S(1)}, u32[]{:S(2)}, u32[]{:S(2)}) collective-permute-start(bf16[4,6,1,192]{3,2,1,0:T(2,128)(2,1)S(1)} %get-tuple-element.25), channel_id=1, source_target_pairs={{0,1},{2,3},{4,5},{6,7},{8,9},{10,11},{12,13},{14,15},{16,17},{18,... | collective-permute-start | bytes 27656 | tf_op jit(solution)/shard_map/ppermute | solution.py:24
  25.8 1.3 %collective-permute-start.4 = (bf16[4,6,1,192]{3,2,1,0:T(2,128)(2,1)S(1)}, bf16[4,6,1,192]{3,2,1,0:T(2,128)(2,1)S(1)}, u32[]{:S(2)}, u32[]{:S(2)}) collective-permute-start(bf16[4,6,1,192]{3,2,1,0:T(2,128)(2,1)S(1)} %get-tuple-element.26), channel_id=1, source_target_pairs={{1,0},{3,2},{5,4},{7,6},{9,8},{11,10},{13,12},{15,14},{17,16},{19,... | collective-permute-start | bytes 27656 | tf_op jit(solution)/shard_map/ppermute | solution.py:26
  27.8 1.1 %collective-permute-done.4 = bf16[4,6,1,192]{3,2,1,0:T(2,128)(2,1)S(1)} collective-permute-done((bf16[4,6,1,192]{3,2,1,0:T(2,128)(2,1)S(1)}, bf16[4,6,1,192]{3,2,1,0:T(2,128)(2,1)S(1)}, u32[]{:S(2)}, u32[]{:S(2)}) %collective-permute-start.4) | collective-permute-done | bytes 9248 | tf_op jit(solution)/shard_map/ppermute | solution.py:26
  28.8 0.4 maximum_maximum_fusion
  29.3 0.6 %fusion.225 = (bf16[2,4,64,192]{3,2,1,0:T(8,128)(2,1)S(1)}, bf16[2,4,64,192]{3,2,1,0:T(8,128)(2,1)S(1)}, bf16[2,4,64,192]{3,2,1,0:T(8,128)(2,1)S(1)}, bf16[2,4,6...) fusion(bf16[4,6,65,192]{3,2,1,0:T(8,128)(2,1)S(1)} %get-tuple-e, ...), kind=kLoop, calls=%fused_computation.297 | loop fusion | bytes 7077888 | tf_op jit(solution)/shard_map/slice | solution.py:45
  37.0 3.5 %collective-permute-start.5 = (bf16[2,1,64,192]{3,2,1,0:T(8,128)(2,1)S(1)}, bf16[2,1,64,192]{3,2,1,0:T(8,128)(2,1)S(1)}, u32[]{:S(2)}, u32[]{:S(2)}) collective-permute-start(bf16[2,1,64,192]{3,2,1,0:T(8,128)(2,1)S(1)} %get-tuple-element.49), channel_id=1, source_target_pairs={{0,4},{4,8},{8,12},{1,5},{5,9},{9,13},{2,6},{6,10},{10,14},{3,7},{... | collective-permute-start | bytes 147464 | tf_op jit(solution)/shard_map/ppermute | solution.py:24
  40.5 1.3 %collective-permute-start.6 = (bf16[2,1,64,192]{3,2,1,0:T(8,128)(2,1)S(1)}, bf16[2,1,64,192]{3,2,1,0:T(8,128)(2,1)S(1)}, u32[]{:S(2)}, u32[]{:S(2)}) collective-permute-start(bf16[2,1,64,192]{3,2,1,0:T(8,128)(2,1)S(1)} %get-tuple-element.50), channel_id=1, source_target_pairs={{4,0},{8,4},{12,8},{5,1},{9,5},{13,9},{6,2},{10,6},{14,10},{7,3},{... | collective-permute-start | bytes 147464 | tf_op jit(solution)/shard_map/ppermute | solution.py:26
  42.4 4.3 %collective-permute-done.6 = bf16[2,1,64,192]{3,2,1,0:T(8,128)(2,1)S(1)} collective-permute-done((bf16[2,1,64,192]{3,2,1,0:T(8,128)(2,1)S(1)}, bf16[2,1,64,192]{3,2,1,0:T(8,128)(2,1)S(1)}, u32[]{:S(2)}, u32[]{:S(2)}) %collective-permute-start.6) | collective-permute-done | bytes 49184 | tf_op jit(solution)/shard_map/ppermute | solution.py:26
  47.2 1.3 %collective-permute-start.7 = (bf16[2,6,1,192]{3,2,1,0:T(2,128)(2,1)S(1)}, bf16[2,6,1,192]{3,2,1,0:T(2,128)(2,1)S(1)}, u32[]{:S(2)}, u32[]{:S(2)}) collective-permute-start(bf16[2,6,1,192]{3,2,1,0:T(2,128)(2,1)S(1)} %get-tuple-element.45), channel_id=1, source_target_pairs={{0,1},{2,3},{4,5},{6,7},{8,9},{10,11},{12,13},{14,15},{16,17},{18,... | collective-permute-start | bytes 13832 | tf_op jit(solution)/shard_map/ppermute | solution.py:24
  48.5 1.3 %collective-permute-start.8 = (bf16[2,6,1,192]{3,2,1,0:T(2,128)(2,1)S(1)}, bf16[2,6,1,192]{3,2,1,0:T(2,128)(2,1)S(1)}, u32[]{:S(2)}, u32[]{:S(2)}) collective-permute-start(bf16[2,6,1,192]{3,2,1,0:T(2,128)(2,1)S(1)} %get-tuple-element.46), channel_id=1, source_target_pairs={{1,0},{3,2},{5,4},{7,6},{9,8},{11,10},{13,12},{15,14},{17,16},{19,... | collective-permute-start | bytes 13832 | tf_op jit(solution)/shard_map/ppermute | solution.py:26
  50.3 1.3 %collective-permute-done.8 = bf16[2,6,1,192]{3,2,1,0:T(2,128)(2,1)S(1)} collective-permute-done((bf16[2,6,1,192]{3,2,1,0:T(2,128)(2,1)S(1)}, bf16[2,6,1,192]{3,2,1,0:T(2,128)(2,1)S(1)}, u32[]{:S(2)}, u32[]{:S(2)}) %collective-permute-start.8) | collective-permute-done | bytes 4640 | tf_op jit(solution)/shard_map/ppermute | solution.py:26
  52.1 0.9 %fusion.120 = f32[512,96]{0,1:T(8,128)} fusion(bf16[512,192]{1,0:T(8,128)(2,1)S(1)} %bitcast.285, bf16[3,3,192,96]{3,2,1,0:T(8,128)(2,1)S(1)} %copy-done), kind=kOutput, calls=%fused_computation.198 | convolution fusion | flops 19003392 | bytes 557056 | tf_op jit(solution)/shard_map/dot_general | solution.py:80
  54.2 0.7 %copy.16 = bf16[512,96]{1,0:T(8,128)(2,1)} copy(bf16[512,96]{0,1:T(8,128)(2,1)S(1)} %fusion.10) | data formatting | bytes 196608 | tf_op jit(solution)/shard_map/convert_element_type | solution.py:81
  56.5 1.1 %convolution_add_fusion.33 = f32[512,96]{0,1:T(8,128)S(1)} fusion(f32[512,96]{0,1:T(8,128)} %fusion.120, bf16[512,192]{1,0:T(8,128)(2,1)S(1)} %bitcast.287, bf16[3,3,192,96]{3,2,1,0:T(8,128)(2,1)S(1)} %copy-done), kind=kOutput, calls=%fused_computation.39 | convolution fusion | flops 18997248 | bytes 753664 | tf_op jit(solution)/shard_map/dot_general | solution.py:79
  60.2 0.8 %copy.20 = bf16[2,4,2,64,192]{4,3,2,1,0:T(8,128)(2,1)} copy(bf16[2,4,2,64,192]{4,3,1,0,2:T(8,128)(2,1)S(1)} %pad_maximum_fusion.2) | data formatting | bytes 786432 | tf_op jit(solution)/shard_map/stack | solution.py:84
  (88 shorter events, 14.8 us)
Async XLA Ops:
  2.3 10.4 %collective-permute-start = (bf16[2,4,64,192]{3,2,1,0:T(8,128)(2,1)S(1)}, bf16[2,4,64,192]{3,2,1,0:T(8,128)(2,1)S(1)}, u32[]{:S(2)}, u32[]{:S(2)}) collective-permute-start(bf16[2,4,64,192]{3,2,1,0:T(8,128)(2,1)S(1)} %fusion.21), channel_id=1, source_target_pairs={{0,2},{1,3},{4,6},{5,7},{8,10},{9,11},{12,14},{13,15},{16,18},{17,... | collective-permute-start | bytes 589832 | tf_op jit(solution)/shard_map/ppermute | solution.py:13
  13.8 6.0 %collective-permute-start.1 = (bf16[4,1,64,192]{3,2,1,0:T(8,128)(2,1)S(1)}, bf16[4,1,64,192]{3,2,1,0:T(8,128)(2,1)S(1)}, u32[]{:S(2)}, u32[]{:S(2)}) collective-permute-start(bf16[4,1,64,192]{3,2,1,0:T(8,128)(2,1)S(1)} %get-tuple-element.35), channel_id=1, source_target_pairs={{0,4},{4,8},{8,12},{1,5},{5,9},{9,13},{2,6},{6,10},{10,14},{3,7},{... | collective-permute-start | bytes 294920 | tf_op jit(solution)/shard_map/ppermute | solution.py:24
  17.3 6.9 %collective-permute-start.2 = (bf16[4,1,64,192]{3,2,1,0:T(8,128)(2,1)S(1)}, bf16[4,1,64,192]{3,2,1,0:T(8,128)(2,1)S(1)}, u32[]{:S(2)}, u32[]{:S(2)}) collective-permute-start(bf16[4,1,64,192]{3,2,1,0:T(8,128)(2,1)S(1)} %get-tuple-element.36), channel_id=1, source_target_pairs={{4,0},{8,4},{12,8},{5,1},{9,5},{13,9},{6,2},{10,6},{14,10},{7,3},{... | collective-permute-start | bytes 294920 | tf_op jit(solution)/shard_map/ppermute | solution.py:26
  24.2 3.3 %copy-start.1 = (bf16[3,3,3,192,192]{4,3,2,1,0:T(8,128)(2,1)S(1)}, bf16[3,3,3,192,192]{4,3,2,1,0:T(8,128)(2,1)}, u32[]{:S(2)}) copy-start(bf16[3,3,3,192,192]{4,3,2,1,0:T(8,128)(2,1)} %param.10) | copy-start | bytes 5971972
  24.2 3.6 %collective-permute-start.3 = (bf16[4,6,1,192]{3,2,1,0:T(2,128)(2,1)S(1)}, bf16[4,6,1,192]{3,2,1,0:T(2,128)(2,1)S(1)}, u32[]{:S(2)}, u32[]{:S(2)}) collective-permute-start(bf16[4,6,1,192]{3,2,1,0:T(2,128)(2,1)S(1)} %get-tuple-element.25), channel_id=1, source_target_pairs={{0,1},{2,3},{4,5},{6,7},{8,9},{10,11},{12,13},{14,15},{16,17},{18,... | collective-permute-start | bytes 27656 | tf_op jit(solution)/shard_map/ppermute | solution.py:24
  25.8 3.1 %collective-permute-start.4 = (bf16[4,6,1,192]{3,2,1,0:T(2,128)(2,1)S(1)}, bf16[4,6,1,192]{3,2,1,0:T(2,128)(2,1)S(1)}, u32[]{:S(2)}, u32[]{:S(2)}) collective-permute-start(bf16[4,6,1,192]{3,2,1,0:T(2,128)(2,1)S(1)} %get-tuple-element.26), channel_id=1, source_target_pairs={{1,0},{3,2},{5,4},{7,6},{9,8},{11,10},{13,12},{15,14},{17,16},{19,... | collective-permute-start | bytes 27656 | tf_op jit(solution)/shard_map/ppermute | solution.py:26
  35.6 1.3 %copy-start.2 = (bf16[2,4,64,192]{3,2,1,0:T(8,128)(2,1)S(1)}, bf16[2,4,64,192]{3,2,1,0:T(8,128)(2,1)}, u32[]{:S(2)}) copy-start(bf16[2,4,64,192]{3,2,1,0:T(8,128)(2,1)} %param.7) | copy-start | bytes 589828
  35.6 1.3 %copy-start.5 = (f32[192]{0:T(256)S(1)}, f32[192]{0:T(256)}, u32[]{:S(2)}) copy-start(f32[192]{0:T(256)} %param.11) | copy-start | bytes 2308
  35.9 5.9 %copy-start = (bf16[3,3,192,96]{3,2,1,0:T(8,128)(2,1)S(1)}, bf16[3,3,192,96]{3,2,1,0:T(8,128)(2,1)}, u32[]{:S(2)}) copy-start(bf16[3,3,192,96]{3,2,1,0:T(8,128)(2,1)} %param.12) | copy-start | bytes 995332
  37.0 5.4 %collective-permute-start.5 = (bf16[2,1,64,192]{3,2,1,0:T(8,128)(2,1)S(1)}, bf16[2,1,64,192]{3,2,1,0:T(8,128)(2,1)S(1)}, u32[]{:S(2)}, u32[]{:S(2)}) collective-permute-start(bf16[2,1,64,192]{3,2,1,0:T(8,128)(2,1)S(1)} %get-tuple-element.49), channel_id=1, source_target_pairs={{0,4},{4,8},{8,12},{1,5},{5,9},{9,13},{2,6},{6,10},{10,14},{3,7},{... | collective-permute-start | bytes 147464 | tf_op jit(solution)/shard_map/ppermute | solution.py:24
  40.5 6.2 %collective-permute-start.6 = (bf16[2,1,64,192]{3,2,1,0:T(8,128)(2,1)S(1)}, bf16[2,1,64,192]{3,2,1,0:T(8,128)(2,1)S(1)}, u32[]{:S(2)}, u32[]{:S(2)}) collective-permute-start(bf16[2,1,64,192]{3,2,1,0:T(8,128)(2,1)S(1)} %get-tuple-element.50), channel_id=1, source_target_pairs={{4,0},{8,4},{12,8},{5,1},{9,5},{13,9},{6,2},{10,6},{14,10},{7,3},{... | collective-permute-start | bytes 147464 | tf_op jit(solution)/shard_map/ppermute | solution.py:26
  47.2 3.0 %collective-permute-start.7 = (bf16[2,6,1,192]{3,2,1,0:T(2,128)(2,1)S(1)}, bf16[2,6,1,192]{3,2,1,0:T(2,128)(2,1)S(1)}, u32[]{:S(2)}, u32[]{:S(2)}) collective-permute-start(bf16[2,6,1,192]{3,2,1,0:T(2,128)(2,1)S(1)} %get-tuple-element.45), channel_id=1, source_target_pairs={{0,1},{2,3},{4,5},{6,7},{8,9},{10,11},{12,13},{14,15},{16,17},{18,... | collective-permute-start | bytes 13832 | tf_op jit(solution)/shard_map/ppermute | solution.py:24
  48.5 3.1 %collective-permute-start.8 = (bf16[2,6,1,192]{3,2,1,0:T(2,128)(2,1)S(1)}, bf16[2,6,1,192]{3,2,1,0:T(2,128)(2,1)S(1)}, u32[]{:S(2)}, u32[]{:S(2)}) collective-permute-start(bf16[2,6,1,192]{3,2,1,0:T(2,128)(2,1)S(1)} %get-tuple-element.46), channel_id=1, source_target_pairs={{1,0},{3,2},{5,4},{7,6},{9,8},{11,10},{13,12},{15,14},{17,16},{19,... | collective-permute-start | bytes 13832 | tf_op jit(solution)/shard_map/ppermute | solution.py:26
  51.8 2.1 %copy-start.4 = (f32[96]{0:T(128)S(1)}, f32[96]{0:T(128)}, u32[]{:S(2)}) copy-start(f32[96]{0:T(128)} %param.13) | copy-start | bytes 1156
  57.9 1.9 %copy-start.3 = (bf16[512,96]{1,0:T(8,128)(2,1)S(1)}, bf16[512,96]{1,0:T(8,128)(2,1)}, u32[]{:S(2)}) copy-start(bf16[512,96]{1,0:T(8,128)(2,1)} %copy.16) | copy-start | bytes 294916
where the time goes:
time: 61.4 us; the launch traced here: 61 us
  starting transfers between devices  19.9 us (32%)
  waiting for transfers between devices  17.8 us (29%)
  matrix products  14.6 us (24%)
  other arithmetic  4.82 us (8%)
  local copies, waits for them, and re-layouts  3.2 us (5%)
  between operations  0.71 us (1%)
    ppermute x4, waiting for transfers between devices, padded_2(): lax.ppermute(head, axis, [((i + 1) % count, i) for i in range(ends)])  11 us
    ppermute x4, starting transfers between devices, padded_2(): lax.ppermute(tail, axis, [(i, (i + 1) % count) for i in range(ends)])  9.82 us
    dot_general x27, matrix products, causal_conv(): jnp.dot(window, weight[a, b, c], preferred_element_type=jnp.float32)  6.8 us
    ppermute x1, waiting for transfers between devices, shifted(): return lax.ppermute(shard, axis, pairs)  5.52 us
    ppermute x4, starting transfers between devices, padded_2(): lax.ppermute(head, axis, [((i + 1) % count, i) for i in range(ends)])  5.17 us
    ppermute x1, starting transfers between devices, shifted(): return lax.ppermute(shard, axis, pairs)  4.89 us
    dot_general x12, matrix products, upsample_conv(): total = total + jnp.dot(window, upper, preferred_element_type=jnp.float32)  3.59 us
    dot_general x12, matrix products, upsample_conv(): total = total + jnp.dot(window, lower, preferred_element_type=jnp.float32)  3.34 us
  transfers between devices with their start and end apart: 9, of which 7 were waited for; matrix products, arithmetic and copies ran while one was open for 3% of the time, Pallas kernels for 0%

commit v1 on v0

v1 whole, which is shorter than its diff:
```python
import functools

import jax
import jax.numpy as jnp
from jax import lax
from jax.experimental import pallas as pl
from jax.experimental.pallas import tpu as pltpu
from jax.sharding import PartitionSpec as P

EPS = 1e-06
EDGE = 16
PHASE_TAPS = (((0, (0,)), (1, (1, 2))), ((1, (0, 1)), (2, (2,))))
F32 = jnp.float32
BF16 = jnp.bfloat16


class Move:
    def __init__(self, src, dst, sems, index, axis, by):
        here = lax.axis_index(axis)
        count = lax.axis_size(axis)
        self.can_send = jnp.logical_and(here + by >= 0, here + by < count)
        self.can_recv = jnp.logical_and(here - by >= 0, here - by < count)
        self.copy = lambda: pltpu.make_async_remote_copy(
            src_ref=src,
            dst_ref=dst,
            send_sem=sems[0].at[index],
            recv_sem=sems[1].at[index],
            device_id={axis: here + by},
            device_id_type=pl.DeviceIdType.MESH,
        )

    def start(self):
        pl.when(self.can_send)(lambda: self.copy().start())

    def recv(self):
        pl.when(self.can_recv)(lambda: self.copy().wait_recv())

    def sent(self):
        pl.when(self.can_send)(lambda: self.copy().wait_send())


def kernel(
    frames, cache, gain, weight, bias, up_weight, up_bias, out,
    fbuf, wbuf, ubuf, folded, ext, res, lbuf, rbuf, lbuf2, rbuf2, mid, low, high,
    local_sems, send_sems, recv_sems,
):
    count, rows, cols, channels = fbuf.shape
    wide = cols + EDGE
    outputs = ubuf.shape[-1]
    sems = (send_sems, recv_sems)
    here = {axis: lax.axis_index(axis) for axis in ("ta", "ha", "wa")}
    first = here["ta"] == 0
    ends = {
        "up": here["ha"] == 0,
        "down": here["ha"] == lax.axis_size("ha") - 1,
        "left": here["wa"] == 0,
        "right": here["wa"] == lax.axis_size("wa") - 1,
    }

    load_frames = pltpu.make_async_copy(frames, fbuf, local_sems.at[0])
    load_weight = pltpu.make_async_copy(weight, wbuf, local_sems.at[1])
    load_up = pltpu.make_async_copy(up_weight, ubuf, local_sems.at[2])
    load_cache = pltpu.make_async_copy(
        cache, ext.at[0:2, 1 : 1 + rows, 0:cols], local_sems.at[3]
    )
    load_frames.start()
    barrier = pltpu.get_barrier_semaphore()
    partners = jnp.int32(0)
    for axis in ("ta", "ha", "wa"):
        for by in (-1, 1):
            there = here[axis] + by
            valid = jnp.logical_and(there >= 0, there < lax.axis_size(axis))

            @pl.when(valid)
            def _():
                pl.semaphore_signal(
                    barrier, inc=1, device_id={axis: there},
                    device_id_type=pl.DeviceIdType.MESH,
                )

            partners = partners + valid.astype(jnp.int32)
    pl.when(first)(load_cache.start)
    load_weight.start()
    load_up.start()

    load_frames.wait()
    for f in range(count):
        for r in range(rows):
            x = fbuf[f, r].astype(F32)
            scale = lax.rsqrt(jnp.mean(x * x, axis=-1, keepdims=True) + EPS)
            v = x * scale * gain[...]
            ext[2 + f, 1 + r, 0:cols] = (v / (1.0 + jnp.exp(-v))).astype(BF16)

    @pl.when(ends["up"])
    def _():
        ext[:, 0, 0:cols] = jnp.zeros((2 + count, cols, channels), BF16)
        res[:, 0, 0:cols] = jnp.zeros((count, cols, channels), BF16)

    @pl.when(ends["down"])
    def _():
        ext[:, 1 + rows, 0:cols] = jnp.zeros((2 + count, cols, channels), BF16)
        res[:, 1 + rows, 0:cols] = jnp.zeros((count, cols, channels), BF16)

    index = 0

    def move(src, dst, axis, by):
        nonlocal index
        made = Move(src, dst, sems, index, axis, by)
        index += 1
        return made

    def row_moves(buf, lo, hi):
        return [
            move(buf.at[lo:hi, 1, 0:cols], buf.at[lo:hi, 1 + rows, 0:cols], "ha", -1),
            move(buf.at[lo:hi, rows, 0:cols], buf.at[lo:hi, 0, 0:cols], "ha", 1),
        ]

    def col_moves(buf, left, right, lo, hi):
        return [
            move(buf.at[lo:hi, :, 0:EDGE], right.at[lo:hi], "wa", -1),
            move(buf.at[lo:hi, :, cols - EDGE : cols], left.at[lo:hi], "wa", 1),
        ]

    def merge(buf, left, right, lo, hi):
        shape = (hi - lo, rows + 2, EDGE, channels)
        at = lax.broadcasted_iota(jnp.int32, shape, 2)
        from_right = jnp.logical_and(at == 0, jnp.logical_not(ends["right"]))
        from_left = jnp.logical_and(at == EDGE - 1, jnp.logical_not(ends["left"]))
        tile = jnp.where(from_left, left[lo:hi].astype(F32), 0.0)
        tile = jnp.where(from_right, right[lo:hi].astype(F32), tile)
        buf[lo:hi, :, cols:wide] = tile.astype(BF16)

    outer = {}
    inner = {}
    for f in (1, 0):
        outer[f] = [
            move(ext.at[2 + f, r, 0:cols], ext.at[f, r, 0:cols], "ta", 1)
            for r in (1, rows)
        ]
    for f in (1, 0):
        inner[f] = move(
            ext.at[2 + f, 2:rows, 0:cols], ext.at[f, 2:rows, 0:cols], "ta", 1
        )
    rows_of = {2: row_moves(ext, 2, 4), 1: row_moves(ext, 1, 2), 0: row_moves(ext, 0, 1)}
    cols_of = {
        2: col_moves(ext, lbuf, rbuf, 2, 4),
        1: col_moves(ext, lbuf, rbuf, 1, 2),
        0: col_moves(ext, lbuf, rbuf, 0, 1),
    }
    rows_res = row_moves(res, 0, count)
    cols_res = col_moves(res, lbuf2, rbuf2, 0, count)

    def each(moves, name):
        for m in moves:
            getattr(m, name)()

    def window(buf, f, start, width):
        return buf[f, start : start + rows, 0:width].reshape(rows * width, channels)

    def center(terms):
        total = None
        for f, a in terms:
            for b in range(3):
                part = jnp.dot(
                    window(ext, f, b, cols), wbuf[9 * a + 3 * b + 1],
                    preferred_element_type=F32,
                )
                total = part if total is None else total + part
        return total

    def side(terms, c):
        total = None
        for f, a in terms:
            for b in range(3):
                part = jnp.dot(
                    window(ext, f, b, wide), wbuf[9 * a + 3 * b + c],
                    preferred_element_type=F32,
                )
                total = part if total is None else total + part
        return total

    own = {0: ((2, 2),), 1: ((2, 1), (3, 2))}

    pl.semaphore_wait(barrier, partners)
    for f in (1, 0):
        each(outer[f], "start")
    each(rows_of[2], "start")
    for f in (1, 0):
        inner[f].start()

    load_up.wait()
    u = {}
    for a in range(3):
        for b in range(3):
            u[a, b] = ubuf[3 * a + b].astype(F32)
    for p in range(2):
        for k in range(2):
            taps = PHASE_TAPS[p][k][1]
            by_col = [functools.reduce(jnp.add, [u[a, b] for a in taps]) for b in range(3)]
            folded[p, k, 0] = jnp.concatenate(
                [by_col[1] + by_col[2], by_col[0] + by_col[1]], axis=-1
            ).astype(BF16)
            folded[p, k, 1] = jnp.concatenate([by_col[0], by_col[2]], axis=-1).astype(BF16)

    each(rows_of[2], "recv")
    each(cols_of[2], "start")
    load_weight.wait()
    for o in (0, 1):
        mid[o] = center(own[o])

    pl.when(first)(load_cache.wait)
    for f in (1, 0):
        each(outer[f], "recv")
        each(rows_of[f], "start")
    each(cols_of[2], "recv")
    merge(ext, lbuf, rbuf, 2, 4)
    for o in (0, 1):
        low[o] = side(own[o], 0)
        high[o] = side(own[o], 2)

    inner[1].recv()
    each(rows_of[1], "recv")
    each(cols_of[1], "start")
    inner[0].recv()
    each(rows_of[0], "recv")
    each(cols_of[0], "start")
    mid[0] += center(((1, 1), (0, 0)))
    mid[1] += center(((1, 0),))
    each(cols_of[1], "recv")
    each(cols_of[0], "recv")
    merge(ext, lbuf, rbuf, 0, 2)

    for o, terms in ((0, ((1, 1), (0, 0))), (1, ((1, 0),))):
        low[o] += side(terms, 0)
        high[o] += side(terms, 2)
        for r in range(rows):
            span = slice(r * wide, (r + 1) * wide)
            total = mid[o, r * cols : (r + 1) * cols]
            total = total + pltpu.roll(low[o, span], 1, 0)[0:cols]
            total = total + pltpu.roll(high[o, span], wide - 1, 0)[0:cols]
            res[o, 1 + r, 0:cols] = (fbuf[o, r].astype(F32) + total + bias[...]).astype(BF16)

    each(rows_res, "start")
    each(rows_res, "recv")
    each(cols_res, "start")
    up = jnp.concatenate([up_bias[...], up_bias[...]], axis=-1)
    lane = lax.broadcasted_iota(jnp.int32, (wide, 2 * outputs), 1)
    for o in range(count):
        for p in range(2):
            total = None
            for k in range(2):
                part = jnp.dot(
                    window(res, o, PHASE_TAPS[p][k][0], cols), folded[p, k, 0],
                    preferred_element_type=F32,
                )
                total = part if total is None else total + part
            if p == 0:
                mid[o] = total
            else:
                high[o, 0 : rows * cols] = total
    each(cols_res, "recv")
    merge(res, lbuf2, rbuf2, 0, count)
    for o in range(count):
        for p in range(2):
            total = None
            for k in range(2):
                part = jnp.dot(
                    window(res, o, PHASE_TAPS[p][k][0], wide), folded[p, k, 1],
                    preferred_element_type=F32,
                )
                total = part if total is None else total + part
            held = mid if p == 0 else high
            for r in range(rows):
                span = total[r * wide : (r + 1) * wide]
                turned = jnp.where(
                    lane < outputs, pltpu.roll(span, 1, 0), pltpu.roll(span, wide - 1, 0)
                )[0:cols]
                value = held[o, r * cols : (r + 1) * cols] + turned + up
                out[o, 2 * r + p] = value.astype(BF16)

    for f in (0, 1):
        each(outer[f], "sent")
        inner[f].sent()
    for f in (0, 1, 2):
        each(rows_of[f], "sent")
        each(cols_of[f], "sent")
    each(rows_res, "sent")
    each(cols_res, "sent")


def on_device(frames, cache, norm_gain, conv_weight, conv_bias, up_weight, up_bias):
    count, rows, cols, channels = frames.shape
    outputs = up_weight.shape[-1]
    wide = cols + EDGE
    moves = 22
    anywhere = pl.BlockSpec(memory_space=pl.ANY)
    vmem = pl.BlockSpec(memory_space=pltpu.VMEM)
    return pl.pallas_call(
        kernel,
        out_shape=jax.ShapeDtypeStruct((count, 2 * rows, cols, 2 * outputs), BF16),
        in_specs=[anywhere, anywhere, vmem, anywhere, vmem, anywhere, vmem],
        out_specs=vmem,
        scratch_shapes=[
            pltpu.VMEM((count, rows, cols, channels), BF16),
            pltpu.VMEM((27, channels, channels), BF16),
            pltpu.VMEM((9, channels, outputs), BF16),
            pltpu.VMEM((2, 2, 2, channels, 2 * outputs), BF16),
            pltpu.VMEM((2 + count, rows + 2, wide, channels), BF16),
            pltpu.VMEM((count, rows + 2, wide, channels), BF16),
            pltpu.VMEM((2 + count, rows + 2, EDGE, channels), BF16),
            pltpu.VMEM((2 + count, rows + 2, EDGE, channels), BF16),
            pltpu.VMEM((count, rows + 2, EDGE, channels), BF16),
            pltpu.VMEM((count, rows + 2, EDGE, channels), BF16),
            pltpu.VMEM((count, rows * cols, channels), F32),
            pltpu.VMEM((count, rows * wide, channels), F32),
            pltpu.VMEM((count, rows * wide, channels), F32),
            pltpu.SemaphoreType.DMA((4,)),
            pltpu.SemaphoreType.DMA((moves,)),
            pltpu.SemaphoreType.DMA((moves,)),
        ],
        compiler_params=pltpu.CompilerParams(
            collective_id=0, has_side_effects=True, vmem_limit_bytes=48 * 1024 * 1024
        ),
        name="level",
    )(
        frames,
        cache,
        norm_gain.reshape(1, channels),
        conv_weight.reshape(27, channels, channels),
        conv_bias.reshape(1, channels),
        up_weight.reshape(9, channels, outputs),
        up_bias.reshape(1, outputs),
    )


def solution(mesh):
    return jax.shard_map(
        on_device,
        mesh=mesh,
        in_specs=(
            P(("clips", "ta"), "ha", "wa", None),
            P("clips", "ha", "wa", None),
            P(),
            P(),
            P(),
            P(),
            P(),
        ),
        out_specs=P(("clips", "ta"), "ha", "wa", None),
        check_vma=False,
    )
```

time: 61.4 us -> 26.9 us (0.44)
  starting transfers between devices: 19.9 us -> 0 us
  Pallas kernels: 0 us -> 19.1 us
  waiting for transfers between devices: 17.8 us -> 0 us
  matrix products: 14.6 us -> 0 us
  other arithmetic: 4.82 us -> 0 us
  local copies, waits for them, and re-layouts: 3.2 us -> 7.47 us
  between operations: 0.71 us -> 0.02 us
    ppermute x9 -> x0, starting transfers between devices: 19.9 us -> none  [the longest x4 9.82 us: padded_2(): lax.ppermute(tail, axis, [(i, (i + 1) % count) for i in range(ends)])]
    pallas_call x0 -> x1, Pallas kernels: none -> 19.1 us  [on_device(): pl.pallas_call(kernel, out_shape=jax.ShapeDtypeStruct((count, 2 * rows, c...]
    ppermute x9 -> x0, waiting for transfers between devices: 17.8 us -> none  [the longest x4 11 us: padded_2(): lax.ppermute(head, axis, [((i + 1) % count, i) for i in range(ends)])]
    dot_general x55 -> x0, matrix products: 14.6 us -> none  [the longest x27 6.8 us: causal_conv(): jnp.dot(window, weight[a, b, c], preferred_element_type=jnp.float32)]
    unnamed x12 -> x15, local copies, waits for them, and re-layouts: 0.04 us -> 7.47 us
    convert_element_type x2 -> x0, other arithmetic: 1.25 us -> none  [the longest x1 1.18 us: activate(): return jax.nn.silu(wide * scale * gain).astype(jnp.bfloat16)]
    convert_element_type x4 -> x0, local copies, waits for them, and re-layouts: 1.1 us -> none  [upsample_conv(): result = (total + bias).astype(jnp.bfloat16)]
    reduce_sum x1 -> x0, other arithmetic: 1.1 us -> none  [activate(): scale = lax.rsqrt(jnp.mean(wide * wide, axis=-1, keepdims=True) + EPS)]
  transfers between devices with their start and end apart: 9 -> 0, of which waited for: 7 -> 0; matrix products, arithmetic and copies ran while one was open for 3% -> 0% of each run, Pallas kernels for 0% -> 0%
where the time goes in v1:
time: 26.9 us; the launch traced here: 26.6 us
  Pallas kernels  19.1 us (71%)
  local copies, waits for them, and re-layouts  7.47 us (28%)
    pallas_call x1, Pallas kernels, on_device(): pl.pallas_call(kernel, out_shape=jax.ShapeDtypeStruct((count, 2 * rows, c...  19.1 us
    unnamed x15, local copies, waits for them, and re-layouts  7.47 us

profile of v1, /device:TPU:0, one launch (start us, length us, event | category | flops | bytes accessed | tf_op | source)
XLA Modules:
  0.0 26.6 jit_solution(14970818967776975966)
XLA Ops:
  0.0 0.0 copy-start
  0.0 1.7 %copy-done = bf16[3,3,3,192,192]{4,3,2,1,0:T(8,128)(2,1)S(1)} copy-done((bf16[3,3,3,192,192]{4,3,2,1,0:T(8,128)(2,1)S(1)}, bf16[3,3,3,192,192]{4,3,2,1,0:T(8,128)(2,1)}, u32[]{:S(2)}) %copy-start) | copy-done | bytes 1990680
  1.8 0.0 copy-start.1
  1.8 1.0 %copy-done.1 = bf16[3,3,192,96]{3,2,1,0:T(8,128)(2,1)S(1)} copy-done((bf16[3,3,192,96]{3,2,1,0:T(8,128)(2,1)S(1)}, bf16[3,3,192,96]{3,2,1,0:T(8,128)(2,1)}, u32[]{:S(2)}) %copy-start.1) | copy-done | bytes 331800
  2.8 0.0 copy-start.2
  2.8 0.9 %copy-done.2 = bf16[2,4,64,192]{3,2,1,0:T(8,128)(2,1)S(1)} copy-done((bf16[2,4,64,192]{3,2,1,0:T(8,128)(2,1)S(1)}, bf16[2,4,64,192]{3,2,1,0:T(8,128)(2,1)}, u32[]{:S(2)}) %copy-start.2) | copy-done | bytes 196632
  3.7 0.0 copy-start.3
  3.7 0.9 %copy-done.3 = bf16[2,4,64,192]{3,2,1,0:T(8,128)(2,1)S(1)} copy-done((bf16[2,4,64,192]{3,2,1,0:T(8,128)(2,1)S(1)}, bf16[2,4,64,192]{3,2,1,0:T(8,128)(2,1)}, u32[]{:S(2)}) %copy-start.3) | copy-done | bytes 196632
  4.7 0.0 copy-start.4
  4.7 0.7 %copy-done.4 = f32[192]{0:T(256)S(1)} copy-done((f32[192]{0:T(256)S(1)}, f32[192]{0:T(256)}, u32[]{:S(2)}) %copy-start.4) | copy-done | bytes 792
  5.3 0.0 copy-start.5
  5.3 0.7 %copy-done.5 = f32[192]{0:T(256)S(1)} copy-done((f32[192]{0:T(256)S(1)}, f32[192]{0:T(256)}, u32[]{:S(2)}) %copy-start.5) | copy-done | bytes 792
  6.0 0.0 copy-start.6
  6.0 0.7 %copy-done.6 = f32[96]{0:T(128)S(1)} copy-done((f32[96]{0:T(128)S(1)}, f32[96]{0:T(128)}, u32[]{:S(2)}) %copy-start.6) | copy-done | bytes 408
  6.7 19.1 %level.1 = bf16[2,8,64,192]{3,2,1,0:T(8,128)(2,1)S(1)} custom-call(bf16[2,4,64,192]{3,2,1,0:T(8,128)(2,1)S(1)} %copy-done.2, bf16[2,4,64,192]{3,2,1,0:T(8,128)(2,1)S(1)} %copy-done.3, f32[1,192]{1,0:T(1,128)S(1)} %bitcast.7, bf16[27,192,192]{2,1,0:T(8,128)(2,1)S(1)} %bitcast.5, f32[1,192]{1,0:T(1,128)S(1)} %bitcast.8, bf16[9,192,96]{2,1,0:T(8,128)(2,1)S(1)} %bitcast.6, ...), custom_call_target="tpu_custom_call" | custom-call | tf_op jit(solution)/shard_map/level/pallas_call | solution.py:298
  25.8 0.8 %copy.9 = bf16[2,8,64,192]{3,2,1,0:T(8,128)(2,1)} copy(bf16[2,8,64,192]{3,2,1,0:T(8,128)(2,1)S(1)} %level.1) | data formatting | bytes 786432
Async XLA Ops:
  0.0 1.7 %copy-start = (bf16[3,3,3,192,192]{4,3,2,1,0:T(8,128)(2,1)S(1)}, bf16[3,3,3,192,192]{4,3,2,1,0:T(8,128)(2,1)}, u32[]{:S(2)}) copy-start(bf16[3,3,3,192,192]{4,3,2,1,0:T(8,128)(2,1)} %param.10) | copy-start | bytes 5971972
  1.8 1.0 %copy-start.1 = (bf16[3,3,192,96]{3,2,1,0:T(8,128)(2,1)S(1)}, bf16[3,3,192,96]{3,2,1,0:T(8,128)(2,1)}, u32[]{:S(2)}) copy-start(bf16[3,3,192,96]{3,2,1,0:T(8,128)(2,1)} %param.12) | copy-start | bytes 995332
  2.8 0.9 %copy-start.2 = (bf16[2,4,64,192]{3,2,1,0:T(8,128)(2,1)S(1)}, bf16[2,4,64,192]{3,2,1,0:T(8,128)(2,1)}, u32[]{:S(2)}) copy-start(bf16[2,4,64,192]{3,2,1,0:T(8,128)(2,1)} %frames.1) | copy-start | bytes 589828
  3.7 0.9 %copy-start.3 = (bf16[2,4,64,192]{3,2,1,0:T(8,128)(2,1)S(1)}, bf16[2,4,64,192]{3,2,1,0:T(8,128)(2,1)}, u32[]{:S(2)}) copy-start(bf16[2,4,64,192]{3,2,1,0:T(8,128)(2,1)} %cache.1) | copy-start | bytes 589828
  4.7 0.7 %copy-start.4 = (f32[192]{0:T(256)S(1)}, f32[192]{0:T(256)}, u32[]{:S(2)}) copy-start(f32[192]{0:T(256)} %param.9) | copy-start | bytes 2308
  5.3 0.7 %copy-start.5 = (f32[192]{0:T(256)S(1)}, f32[192]{0:T(256)}, u32[]{:S(2)}) copy-start(f32[192]{0:T(256)} %param.11) | copy-start | bytes 2308
  6.0 0.7 %copy-start.6 = (f32[96]{0:T(128)S(1)}, f32[96]{0:T(128)}, u32[]{:S(2)}) copy-start(f32[96]{0:T(128)} %param.13) | copy-start | bytes 1156

commit v2 on v1

--- a/solution.py
+++ b/solution.py
@@ -40,8 +40,8 @@
 
 
 def kernel(
-    frames, cache, gain, weight, bias, up_weight, up_bias, out,
-    fbuf, wbuf, ubuf, folded, ext, res, lbuf, rbuf, lbuf2, rbuf2, mid, low, high,
+    frames, cache, gain_in, weight, bias_in, up_weight, up_bias_in, out,
+    fbuf, wbuf, ubuf, gain, bias, up_bias, folded, ext, res, lbuf, rbuf, lbuf2, rbuf2, mid, low, high,
     local_sems, send_sems, recv_sems,
 ):
     count, rows, cols, channels = fbuf.shape
@@ -63,7 +63,11 @@
     load_cache = pltpu.make_async_copy(
         cache, ext.at[0:2, 1 : 1 + rows, 0:cols], local_sems.at[3]
     )
+    load_gain = pltpu.make_async_copy(gain_in, gain, local_sems.at[4])
+    load_bias = pltpu.make_async_copy(bias_in, bias, local_sems.at[5])
+    load_up_bias = pltpu.make_async_copy(up_bias_in, up_bias, local_sems.at[6])
     load_frames.start()
+    load_gain.start()
     barrier = pltpu.get_barrier_semaphore()
     partners = jnp.int32(0)
     for axis in ("ta", "ha", "wa"):
@@ -82,7 +86,10 @@
     pl.when(first)(load_cache.start)
     load_weight.start()
     load_up.start()
-
+    load_bias.start()
+    load_up_bias.start()
+
+    load_gain.wait()
     load_frames.wait()
     for f in range(count):
         for r in range(rows):
@@ -189,6 +196,8 @@
         inner[f].start()
 
     load_up.wait()
+    load_bias.wait()
+    load_up_bias.wait()
     u = {}
     for a in range(3):
         for b in range(3):
@@ -293,17 +302,20 @@
     outputs = up_weight.shape[-1]
     wide = cols + EDGE
     moves = 22
-    anywhere = pl.BlockSpec(memory_space=pl.ANY)
+    hbm = pl.BlockSpec(memory_space=pltpu.HBM)
     vmem = pl.BlockSpec(memory_space=pltpu.VMEM)
     return pl.pallas_call(
         kernel,
         out_shape=jax.ShapeDtypeStruct((count, 2 * rows, cols, 2 * outputs), BF16),
-        in_specs=[anywhere, anywhere, vmem, anywhere, vmem, anywhere, vmem],
+        in_specs=[hbm] * 7,
         out_specs=vmem,
         scratch_shapes=[
             pltpu.VMEM((count, rows, cols, channels), BF16),
             pltpu.VMEM((27, channels, channels), BF16),
             pltpu.VMEM((9, channels, outputs), BF16),
+            pltpu.VMEM((1, channels), F32),
+            pltpu.VMEM((1, channels), F32),
+            pltpu.VMEM((1, outputs), F32),
             pltpu.VMEM((2, 2, 2, channels, 2 * outputs), BF16),
             pltpu.VMEM((2 + count, rows + 2, wide, channels), BF16),
             pltpu.VMEM((count, rows + 2, wide, channels), BF16),
@@ -314,7 +326,7 @@
             pltpu.VMEM((count, rows * cols, channels), F32),
             pltpu.VMEM((count, rows * wide, channels), F32),
             pltpu.VMEM((count, rows * wide, channels), F32),
-            pltpu.SemaphoreType.DMA((4,)),
+            pltpu.SemaphoreType.DMA((7,)),
             pltpu.SemaphoreType.DMA((moves,)),
             pltpu.SemaphoreType.DMA((moves,)),
         ],

time: 26.9 us -> 26.9 us (level)
  no operation moved by 1% of the time
where the time goes in v2:
time: 26.9 us; the launch traced here: 26.7 us
  Pallas kernels  19.2 us (71%)
  local copies, waits for them, and re-layouts  7.47 us (28%)
    pallas_call x1, Pallas kernels, on_device(): pl.pallas_call(kernel, out_shape=jax.ShapeDtypeStruct((count, 2 * rows, c...  19.2 us
    unnamed x15, local copies, waits for them, and re-layouts  7.47 us

profile of v2, /device:TPU:0, one launch (start us, length us, event | category | flops | bytes accessed | tf_op | source)
XLA Modules:
  0.0 26.7 jit_solution(4951581941505236979)
XLA Ops:
  0.0 0.0 copy-start
  0.0 1.7 %copy-done = bf16[3,3,3,192,192]{4,3,2,1,0:T(8,128)(2,1)S(1)} copy-done((bf16[3,3,3,192,192]{4,3,2,1,0:T(8,128)(2,1)S(1)}, bf16[3,3,3,192,192]{4,3,2,1,0:T(8,128)(2,1)}, u32[]{:S(2)}) %copy-start) | copy-done | bytes 1990680
  1.8 0.0 copy-start.1
  1.8 1.0 %copy-done.1 = bf16[3,3,192,96]{3,2,1,0:T(8,128)(2,1)S(1)} copy-done((bf16[3,3,192,96]{3,2,1,0:T(8,128)(2,1)S(1)}, bf16[3,3,192,96]{3,2,1,0:T(8,128)(2,1)}, u32[]{:S(2)}) %copy-start.1) | copy-done | bytes 331800
  2.8 0.0 copy-start.2
  2.8 0.9 %copy-done.2 = bf16[2,4,64,192]{3,2,1,0:T(8,128)(2,1)S(1)} copy-done((bf16[2,4,64,192]{3,2,1,0:T(8,128)(2,1)S(1)}, bf16[2,4,64,192]{3,2,1,0:T(8,128)(2,1)}, u32[]{:S(2)}) %copy-start.2) | copy-done | bytes 196632
  3.7 0.0 copy-start.3
  3.7 0.9 %copy-done.3 = bf16[2,4,64,192]{3,2,1,0:T(8,128)(2,1)S(1)} copy-done((bf16[2,4,64,192]{3,2,1,0:T(8,128)(2,1)S(1)}, bf16[2,4,64,192]{3,2,1,0:T(8,128)(2,1)}, u32[]{:S(2)}) %copy-start.3) | copy-done | bytes 196632
  4.7 0.0 copy-start.4
  4.7 0.7 %copy-done.4 = f32[192]{0:T(256)S(1)} copy-done((f32[192]{0:T(256)S(1)}, f32[192]{0:T(256)}, u32[]{:S(2)}) %copy-start.4) | copy-done | bytes 792
  5.3 0.0 copy-start.5
  5.3 0.7 %copy-done.5 = f32[192]{0:T(256)S(1)} copy-done((f32[192]{0:T(256)S(1)}, f32[192]{0:T(256)}, u32[]{:S(2)}) %copy-start.5) | copy-done | bytes 792
  6.0 0.0 copy-start.6
  6.0 0.7 %copy-done.6 = f32[96]{0:T(128)S(1)} copy-done((f32[96]{0:T(128)S(1)}, f32[96]{0:T(128)}, u32[]{:S(2)}) %copy-start.6) | copy-done | bytes 408
  6.7 19.2 %level.1 = bf16[2,8,64,192]{3,2,1,0:T(8,128)(2,1)S(1)} custom-call(bf16[2,4,64,192]{3,2,1,0:T(8,128)(2,1)S(1)} %copy-done.2, bf16[2,4,64,192]{3,2,1,0:T(8,128)(2,1)S(1)} %copy-done.3, f32[1,192]{1,0:T(1,128)S(1)} %bitcast.7, bf16[27,192,192]{2,1,0:T(8,128)(2,1)S(1)} %bitcast.5, f32[1,192]{1,0:T(1,128)S(1)} %bitcast.8, bf16[9,192,96]{2,1,0:T(8,128)(2,1)S(1)} %bitcast.6, ...), custom_call_target="tpu_custom_call" | custom-call | tf_op jit(solution)/shard_map/level/pallas_call | solution.py:307
  25.9 0.8 %copy.9 = bf16[2,8,64,192]{3,2,1,0:T(8,128)(2,1)} copy(bf16[2,8,64,192]{3,2,1,0:T(8,128)(2,1)S(1)} %level.1) | data formatting | bytes 786432
Async XLA Ops:
  0.0 1.7 %copy-start = (bf16[3,3,3,192,192]{4,3,2,1,0:T(8,128)(2,1)S(1)}, bf16[3,3,3,192,192]{4,3,2,1,0:T(8,128)(2,1)}, u32[]{:S(2)}) copy-start(bf16[3,3,3,192,192]{4,3,2,1,0:T(8,128)(2,1)} %param.10) | copy-start | bytes 5971972
  1.8 1.0 %copy-start.1 = (bf16[3,3,192,96]{3,2,1,0:T(8,128)(2,1)S(1)}, bf16[3,3,192,96]{3,2,1,0:T(8,128)(2,1)}, u32[]{:S(2)}) copy-start(bf16[3,3,192,96]{3,2,1,0:T(8,128)(2,1)} %param.12) | copy-start | bytes 995332
  2.8 0.9 %copy-start.2 = (bf16[2,4,64,192]{3,2,1,0:T(8,128)(2,1)S(1)}, bf16[2,4,64,192]{3,2,1,0:T(8,128)(2,1)}, u32[]{:S(2)}) copy-start(bf16[2,4,64,192]{3,2,1,0:T(8,128)(2,1)} %frames.1) | copy-start | bytes 589828
  3.7 0.9 %copy-start.3 = (bf16[2,4,64,192]{3,2,1,0:T(8,128)(2,1)S(1)}, bf16[2,4,64,192]{3,2,1,0:T(8,128)(2,1)}, u32[]{:S(2)}) copy-start(bf16[2,4,64,192]{3,2,1,0:T(8,128)(2,1)} %cache.1) | copy-start | bytes 589828
  4.7 0.7 %copy-start.4 = (f32[192]{0:T(256)S(1)}, f32[192]{0:T(256)}, u32[]{:S(2)}) copy-start(f32[192]{0:T(256)} %param.9) | copy-start | bytes 2308
  5.3 0.7 %copy-start.5 = (f32[192]{0:T(256)S(1)}, f32[192]{0:T(256)}, u32[]{:S(2)}) copy-start(f32[192]{0:T(256)} %param.11) | copy-start | bytes 2308
  6.0 0.7 %copy-start.6 = (f32[96]{0:T(128)S(1)}, f32[96]{0:T(128)}, u32[]{:S(2)}) copy-start(f32[96]{0:T(128)} %param.13) | copy-start | bytes 1156

commit v3 on v2

v3 whole, which is shorter than its diff:
```python
import functools

import jax
import jax.numpy as jnp
from jax import lax
from jax.experimental import pallas as pl
from jax.experimental.pallas import tpu as pltpu
from jax.sharding import PartitionSpec as P

EPS = 1e-06
EDGE = 16
PHASE_TAPS = (((0, (0,)), (1, (1, 2))), ((1, (0, 1)), (2, (2,))))
NEIGHBOURS = (
    {"ta": 1}, {"ta": -1}, {"ha": 1}, {"ha": -1}, {"wa": 1}, {"wa": -1},
    {"ha": 1, "wa": 1}, {"ha": 1, "wa": -1}, {"ha": -1, "wa": 1}, {"ha": -1, "wa": -1},
)
F32 = jnp.float32
BF16 = jnp.bfloat16


def reachable(by, sign):
    found = None
    for axis, step in by.items():
        there = lax.axis_index(axis) + sign * step
        inside = jnp.logical_and(there >= 0, there < lax.axis_size(axis))
        found = inside if found is None else jnp.logical_and(found, inside)
    return found


class Move:
    def __init__(self, src, dst, sems, index, by):
        self.can_send = reachable(by, 1)
        self.can_recv = reachable(by, -1)
        self.copy = lambda: pltpu.make_async_remote_copy(
            src_ref=src,
            dst_ref=dst,
            send_sem=sems[0].at[index],
            recv_sem=sems[1].at[index],
            device_id={axis: lax.axis_index(axis) + step for axis, step in by.items()},
            device_id_type=pl.DeviceIdType.MESH,
        )

    def start(self):
        pl.when(self.can_send)(lambda: self.copy().start())

    def recv(self):
        pl.when(self.can_recv)(lambda: self.copy().wait_recv())

    def sent(self):
        pl.when(self.can_send)(lambda: self.copy().wait_send())


def kernel(
    frames, cache, gain_in, weight, bias_in, up_weight, up_bias_in, out,
    fbuf, wbuf, ubuf, gain, bias, up_bias, folded, ext, res, lbuf, rbuf, lbuf2, rbuf2, mid, low, high, obuf,
    local_sems, send_sems, recv_sems,
):
    count, rows, cols, channels = fbuf.shape
    wide = cols + EDGE
    outputs = ubuf.shape[-1]
    sems = (send_sems, recv_sems)
    here = {axis: lax.axis_index(axis) for axis in ("ta", "ha", "wa")}
    first = here["ta"] == 0
    ends = {
        "up": here["ha"] == 0,
        "down": here["ha"] == lax.axis_size("ha") - 1,
        "left": here["wa"] == 0,
        "right": here["wa"] == lax.axis_size("wa") - 1,
    }

    load_frames = pltpu.make_async_copy(frames, fbuf, local_sems.at[0])
    load_weight = pltpu.make_async_copy(weight, wbuf, local_sems.at[1])
    load_up = pltpu.make_async_copy(up_weight, ubuf, local_sems.at[2])
    load_cache = pltpu.make_async_copy(
        cache, ext.at[0:2, 1 : 1 + rows, 0:cols], local_sems.at[3]
    )
    load_gain = pltpu.make_async_copy(gain_in, gain, local_sems.at[4])
    load_bias = pltpu.make_async_copy(bias_in, bias, local_sems.at[5])
    load_up_bias = pltpu.make_async_copy(up_bias_in, up_bias, local_sems.at[6])
    load_frames.start()
    load_gain.start()
    barrier = pltpu.get_barrier_semaphore()
    partners = jnp.int32(0)
    for by in NEIGHBOURS:
        valid = reachable(by, 1)

        @pl.when(valid)
        def _():
            pl.semaphore_signal(
                barrier, inc=1,
                device_id={axis: here[axis] + step for axis, step in by.items()},
                device_id_type=pl.DeviceIdType.MESH,
            )

        partners = partners + valid.astype(jnp.int32)
    pl.when(first)(load_cache.start)
    load_weight.start()
    load_up.start()
    load_bias.start()
    load_up_bias.start()

    load_gain.wait()
    load_frames.wait()
    for f in range(count):
        for r in range(rows):
            x = fbuf[f, r].astype(F32)
            scale = lax.rsqrt(jnp.mean(x * x, axis=-1, keepdims=True) + EPS)
            v = x * scale * gain[...]
            ext[2 + f, 1 + r, 0:cols] = (v / (1.0 + jnp.exp(-v))).astype(BF16)

    @pl.when(ends["up"])
    def _():
        ext[:, 0, 0:cols] = jnp.zeros((2 + count, cols, channels), BF16)
        res[:, 0, 0:cols] = jnp.zeros((count, cols, channels), BF16)

    @pl.when(ends["down"])
    def _():
        ext[:, 1 + rows, 0:cols] = jnp.zeros((2 + count, cols, channels), BF16)
        res[:, 1 + rows, 0:cols] = jnp.zeros((count, cols, channels), BF16)

    index = 0

    def move(src, dst, by):
        nonlocal index
        made = Move(src, dst, sems, index, by)
        index += 1
        return made

    last = cols - EDGE

    def edges(buf, left, right, lo, hi):
        inside = slice(1, 1 + rows)
        near = slice(0, EDGE)
        far = slice(last, cols)
        across = [
            move(buf.at[lo:hi, 1, 0:cols], buf.at[lo:hi, 1 + rows, 0:cols], {"ha": -1}),
            move(buf.at[lo:hi, rows, 0:cols], buf.at[lo:hi, 0, 0:cols], {"ha": 1}),
        ]
        beside = [
            move(buf.at[lo:hi, 1, near], right.at[lo:hi, 1 + rows], {"ha": -1, "wa": -1}),
            move(buf.at[lo:hi, 1, far], left.at[lo:hi, 1 + rows], {"ha": -1, "wa": 1}),
            move(buf.at[lo:hi, rows, near], right.at[lo:hi, 0], {"ha": 1, "wa": -1}),
            move(buf.at[lo:hi, rows, far], left.at[lo:hi, 0], {"ha": 1, "wa": 1}),
            move(buf.at[lo:hi, inside, near], right.at[lo:hi, inside], {"wa": -1}),
            move(buf.at[lo:hi, inside, far], left.at[lo:hi, inside], {"wa": 1}),
        ]
        return across, beside

    def merge(buf, left, right, lo, hi):
        shape = (hi - lo, rows + 2, EDGE, channels)
        row = lax.broadcasted_iota(jnp.int32, shape, 1)
        at = lax.broadcasted_iota(jnp.int32, shape, 2)
        top = jnp.where(ends["up"], 1, 0)
        end = jnp.where(ends["down"], rows, rows + 1)
        held = jnp.logical_and(row >= top, row <= end)
        near = jnp.where(ends["right"], -1, 0)
        far = jnp.where(ends["left"], -1, EDGE - 1)
        tile = jnp.where(jnp.logical_and(held, at == far), left[lo:hi].astype(F32), 0.0)
        tile = jnp.where(jnp.logical_and(held, at == near), right[lo:hi].astype(F32), tile)
        buf[lo:hi, :, cols:wide] = tile.astype(BF16)

    def later(at, row, col):
        return move(ext.at[(at[0],) + (row, col)], ext.at[(at[1],) + (row, col)], {"ta": 1})

    both = (slice(2, 4), slice(0, 2))
    outer = [
        later(both, 1, slice(0, cols)),
        later(both, rows, slice(0, cols)),
        later(both, slice(2, rows), slice(0, EDGE)),
        later(both, slice(2, rows), slice(last, cols)),
    ]
    inner = {f: later((2 + f, f), slice(2, rows), slice(EDGE, last)) for f in (1, 0)}
    across_own, beside_own = edges(ext, lbuf, rbuf, 2, 4)
    across_old, beside_old = edges(ext, lbuf, rbuf, 0, 2)
    across_res, beside_res = {}, {}
    for o in (1, 0):
        across_res[o], beside_res[o] = edges(res, lbuf2, rbuf2, o, o + 1)

    def each(moves, name):
        for m in moves:
            getattr(m, name)()

    def window(buf, f, start, width):
        return buf[f, start : start + rows, 0:width].reshape(rows * width, channels)

    def center(terms):
        total = None
        for f, a in terms:
            for b in range(3):
                part = jnp.dot(
                    window(ext, f, b, cols), wbuf[9 * a + 3 * b + 1],
                    preferred_element_type=F32,
                )
                total = part if total is None else total + part
        return total

    def side(terms, c):
        total = None
        for f, a in terms:
            for b in range(3):
                part = jnp.dot(
                    window(ext, f, b, wide), wbuf[9 * a + 3 * b + c],
                    preferred_element_type=F32,
                )
                total = part if total is None else total + part
        return total

    own = {0: ((2, 2),), 1: ((2, 1), (3, 2))}

    pl.semaphore_wait(barrier, partners)
    each(outer, "start")
    each(across_own, "start")
    each(beside_own, "start")
    for f in (1, 0):
        inner[f].start()

    load_up.wait()
    load_bias.wait()
    load_up_bias.wait()
    u = {}
    for a in range(3):
        for b in range(3):
            u[a, b] = ubuf[3 * a + b].astype(F32)
    for p in range(2):
        for k in range(2):
            taps = PHASE_TAPS[p][k][1]
            by_col = [functools.reduce(jnp.add, [u[a, b] for a in taps]) for b in range(3)]
            folded[p, k, 0] = jnp.concatenate(
                [by_col[1] + by_col[2], by_col[0] + by_col[1]], axis=-1
            ).astype(BF16)
            folded[p, k, 1] = jnp.concatenate([by_col[0], by_col[2]], axis=-1).astype(BF16)

    load_weight.wait()
    each(across_own, "recv")
    for o in (1, 0):
        mid[o] = center(own[o])
    each(beside_own, "recv")
    merge(ext, lbuf, rbuf, 2, 4)
    low[1] = side(own[1], 0)
    high[1] = side(own[1], 2)

    pl.when(first)(load_cache.wait)
    each(outer, "recv")
    each(across_old, "start")
    each(beside_old, "start")
    low[0] = side(own[0], 0)
    high[0] = side(own[0], 2)

    def finish(o, center_sum, low_sum, high_sum):
        for r in range(rows):
            span = slice(r * wide, (r + 1) * wide)
            total = center_sum[r * cols : (r + 1) * cols]
            total = total + pltpu.roll(low_sum[span], 1, 0)[0:cols]
            total = total + pltpu.roll(high_sum[span], wide - 1, 0)[0:cols]
            res[o, 1 + r, 0:cols] = (fbuf[o, r].astype(F32) + total + bias[...]).astype(BF16)

    inner[1].recv()
    each(across_old, "recv")
    mid[1] += center(((1, 0),))
    each(beside_old, "recv")
    merge(ext, lbuf, rbuf, 0, 2)
    low[1] += side(((1, 0),), 0)
    high[1] += side(((1, 0),), 2)
    finish(1, mid.at[1], low.at[1], high.at[1])
    each(across_res[1], "start")
    each(beside_res[1], "start")

    inner[0].recv()
    mid[0] += center(((1, 1), (0, 0)))
    low[0] += side(((1, 1), (0, 0)), 0)
    high[0] += side(((1, 1), (0, 0)), 2)
    finish(0, mid.at[0], low.at[0], high.at[0])
    each(across_res[0], "start")
    each(beside_res[0], "start")

    up = jnp.concatenate([up_bias[...], up_bias[...]], axis=-1)
    lane = lax.broadcasted_iota(jnp.int32, (wide, 2 * outputs), 1)

    def raised(o, p, kind, width):
        total = None
        for k in range(2):
            part = jnp.dot(
                window(res, o, PHASE_TAPS[p][k][0], width), folded[p, k, kind],
                preferred_element_type=F32,
            )
            total = part if total is None else total + part
        return total

    stores = {o: pltpu.make_async_copy(obuf.at[o], out.at[o], local_sems.at[7 + o]) for o in (1, 0)}
    for o in (1, 0):
        each(across_res[o], "recv")
        mid[o] = raised(o, 0, 0, cols)
        high[o, 0 : rows * cols] = raised(o, 1, 0, cols)
        each(beside_res[o], "recv")
        merge(res, lbuf2, rbuf2, o, o + 1)
        for p in range(2):
            total = raised(o, p, 1, wide)
            held = mid if p == 0 else high
            for r in range(rows):
                span = total[r * wide : (r + 1) * wide]
                turned = jnp.where(
                    lane < outputs, pltpu.roll(span, 1, 0), pltpu.roll(span, wide - 1, 0)
                )[0:cols]
                value = held[o, r * cols : (r + 1) * cols] + turned + up
                obuf[o, 2 * r + p] = value.astype(BF16)
        stores[o].start()

    each(outer, "sent")
    for f in (1, 0):
        inner[f].sent()
    for moves in (across_own, beside_own, across_old, beside_old):
        each(moves, "sent")
    for o in (1, 0):
        each(across_res[o], "sent")
        each(beside_res[o], "sent")
        stores[o].wait()


def on_device(frames, cache, norm_gain, conv_weight, conv_bias, up_weight, up_bias):
    count, rows, cols, channels = frames.shape
    outputs = up_weight.shape[-1]
    wide = cols + EDGE
    moves = 38
    hbm = pl.BlockSpec(memory_space=pltpu.HBM)
    return pl.pallas_call(
        kernel,
        out_shape=jax.ShapeDtypeStruct((count, 2 * rows, cols, 2 * outputs), BF16),
        in_specs=[hbm] * 7,
        out_specs=hbm,
        scratch_shapes=[
            pltpu.VMEM((count, rows, cols, channels), BF16),
            pltpu.VMEM((27, channels, channels), BF16),
            pltpu.VMEM((9, channels, outputs), BF16),
            pltpu.VMEM((1, channels), F32),
            pltpu.VMEM((1, channels), F32),
            pltpu.VMEM((1, outputs), F32),
            pltpu.VMEM((2, 2, 2, channels, 2 * outputs), BF16),
            pltpu.VMEM((2 + count, rows + 2, wide, channels), BF16),
            pltpu.VMEM((count, rows + 2, wide, channels), BF16),
            pltpu.VMEM((2 + count, rows + 2, EDGE, channels), BF16),
            pltpu.VMEM((2 + count, rows + 2, EDGE, channels), BF16),
            pltpu.VMEM((count, rows + 2, EDGE, channels), BF16),
            pltpu.VMEM((count, rows + 2, EDGE, channels), BF16),
            pltpu.VMEM((count, rows * cols, channels), F32),
            pltpu.VMEM((count, rows * wide, channels), F32),
            pltpu.VMEM((count, rows * wide, channels), F32),
            pltpu.VMEM((count, 2 * rows, cols, 2 * outputs), BF16),
            pltpu.SemaphoreType.DMA((9,)),
            pltpu.SemaphoreType.DMA((moves,)),
            pltpu.SemaphoreType.DMA((moves,)),
        ],
        compiler_params=pltpu.CompilerParams(
            collective_id=0, has_side_effects=True, vmem_limit_bytes=65_000_000
        ),
        name="level",
    )(
        frames,
        cache,
        norm_gain.reshape(1, channels),
        conv_weight.reshape(27, channels, channels),
        conv_bias.reshape(1, channels),
        up_weight.reshape(9, channels, outputs),
        up_bias.reshape(1, outputs),
    )


def solution(mesh):
    return jax.shard_map(
        on_device,
        mesh=mesh,
        in_specs=(
            P(("clips", "ta"), "ha", "wa", None),
            P("clips", "ha", "wa", None),
            P(),
            P(),
            P(),
            P(),
            P(),
        ),
        out_specs=P(("clips", "ta"), "ha", "wa", None),
        check_vma=False,
    )
```

time: 26.9 us -> 21.4 us (0.80)
  local copies, waits for them, and re-layouts: 7.47 us -> 1.88 us
    unnamed x15 -> x1, local copies, waits for them, and re-layouts: 7.47 us -> 1.88 us
where the time goes in v3:
time: 21.4 us; the launch traced here: 21.2 us
  Pallas kernels  19.4 us (91%)
  local copies, waits for them, and re-layouts  1.88 us (9%)
    pallas_call x1, Pallas kernels, on_device(): pl.pallas_call(kernel, out_shape=jax.ShapeDtypeStruct((count, 2 * rows, c...  19.4 us
    unnamed x1, local copies, waits for them, and re-layouts  1.88 us

profile of v3, /device:TPU:0, one launch (start us, length us, event | category | flops | bytes accessed | tf_op | source)
XLA Modules:
  0.0 21.2 jit_solution(9198532057423635242)
XLA Ops:
  0.0 19.4 %level.1 = bf16[2,8,64,192]{3,2,1,0:T(8,128)(2,1)} custom-call(bf16[2,4,64,192]{3,2,1,0:T(8,128)(2,1)} %frames.1, bf16[2,4,64,192]{3,2,1,0:T(8,128)(2,1)} %cache.1, f32[1,192]{1,0:T(1,128)} %bitcast.7, bf16[27,192,192]{2,1,0:T(8,128)(2,1)} %bitcast.5, f32[1,192]{1,0:T(1,128)} %bitcast.8, bf16[9,192,96]{2,1,0:T(8,128)(2,1)} %bitcast.6, f32[1,96]{1,0:T(1,128)} %bitcast.9), custom_call_target="tpu_custom_call" | custom-call | tf_op jit(solution)/shard_map/level/pallas_call | solution.py:325
  19.4 1.9 %copy.9 = bf16[2,8,64,192]{3,2,1,0:T(8,128)(2,1)} copy(bf16[2,8,64,192]{3,2,1,0:T(8,128)(2,1)} %level.1) | data formatting | bytes 786432

commit v4 on v3

--- a/solution.py
+++ b/solution.py
@@ -230,6 +230,12 @@
             ).astype(BF16)
             folded[p, k, 1] = jnp.concatenate([by_col[0], by_col[2]], axis=-1).astype(BF16)
 
+    pl.when(first)(load_cache.wait)
+    for k in range(2):
+        outer[k].recv()
+        across_old[k].start()
+    each(outer[2:], "recv")
+    each(beside_old, "start")
     load_weight.wait()
     each(across_own, "recv")
     for o in (1, 0):
@@ -239,10 +245,6 @@
     low[1] = side(own[1], 0)
     high[1] = side(own[1], 2)
 
-    pl.when(first)(load_cache.wait)
-    each(outer, "recv")
-    each(across_old, "start")
-    each(beside_old, "start")
     low[0] = side(own[0], 0)
     high[0] = side(own[0], 2)
 

time: 21.4 us -> 19.5 us (0.911)
  the two profiles are of different devices: /device:TPU:0 before, /device:TPU:3 now
where the time goes in v4:
time: 19.5 us; the launch traced here: 19.4 us
  Pallas kernels  17.5 us (90%)
  local copies, waits for them, and re-layouts  1.88 us (10%)
    pallas_call x1, Pallas kernels, on_device(): pl.pallas_call(kernel, out_shape=jax.ShapeDtypeStruct((count, 2 * rows, c...  17.5 us
    unnamed x1, local copies, waits for them, and re-layouts  1.88 us

profile of v4, /device:TPU:3, one launch (start us, length us, event | category | flops | bytes accessed | tf_op | source)
XLA Modules:
  0.0 19.4 jit_solution(18382791913999844742)
XLA Ops:
  0.0 17.5 %level.1 = bf16[2,8,64,192]{3,2,1,0:T(8,128)(2,1)} custom-call(bf16[2,4,64,192]{3,2,1,0:T(8,128)(2,1)} %frames.1, bf16[2,4,64,192]{3,2,1,0:T(8,128)(2,1)} %cache.1, f32[1,192]{1,0:T(1,128)} %bitcast.7, bf16[27,192,192]{2,1,0:T(8,128)(2,1)} %bitcast.5, f32[1,192]{1,0:T(1,128)} %bitcast.8, bf16[9,192,96]{2,1,0:T(8,128)(2,1)} %bitcast.6, f32[1,96]{1,0:T(1,128)} %bitcast.9), custom_call_target="tpu_custom_call" | custom-call | tf_op jit(solution)/shard_map/level/pallas_call | solution.py:327
  17.5 1.9 %copy.9 = bf16[2,8,64,192]{3,2,1,0:T(8,128)(2,1)} copy(bf16[2,8,64,192]{3,2,1,0:T(8,128)(2,1)} %level.1) | data formatting | bytes 786432

commit v5 on v4

--- a/solution.py
+++ b/solution.py
@@ -101,12 +101,15 @@
 
     load_gain.wait()
     load_frames.wait()
+    def activate(f, r):
+        x = fbuf[f, r].astype(F32)
+        scale = lax.rsqrt(jnp.mean(x * x, axis=-1, keepdims=True) + EPS)
+        v = x * scale * gain[...]
+        ext[2 + f, 1 + r, 0:cols] = (v / (1.0 + jnp.exp(-v))).astype(BF16)
+
     for f in range(count):
-        for r in range(rows):
-            x = fbuf[f, r].astype(F32)
-            scale = lax.rsqrt(jnp.mean(x * x, axis=-1, keepdims=True) + EPS)
-            v = x * scale * gain[...]
-            ext[2 + f, 1 + r, 0:cols] = (v / (1.0 + jnp.exp(-v))).astype(BF16)
+        for r in (0, rows - 1):
+            activate(f, r)
 
     @pl.when(ends["up"])
     def _():
@@ -208,9 +211,14 @@
     own = {0: ((2, 2),), 1: ((2, 1), (3, 2))}
 
     pl.semaphore_wait(barrier, partners)
-    each(outer, "start")
+    each(outer[:2], "start")
     each(across_own, "start")
-    each(beside_own, "start")
+    each(beside_own[:4], "start")
+    for f in range(count):
+        for r in range(1, rows - 1):
+            activate(f, r)
+    each(outer[2:], "start")
+    each(beside_own[4:], "start")
     for f in (1, 0):
         inner[f].start()
 

time: 19.5 us -> 19.5 us (level)
  no operation moved by 1% of the time
where the time goes in v5:
time: 19.5 us; the launch traced here: 19.4 us
  Pallas kernels  17.5 us (90%)
  local copies, waits for them, and re-layouts  1.88 us (10%)
    pallas_call x1, Pallas kernels, on_device(): pl.pallas_call(kernel, out_shape=jax.ShapeDtypeStruct((count, 2 * rows, c...  17.5 us
    unnamed x1, local copies, waits for them, and re-layouts  1.88 us

profile of v5, /device:TPU:3, one launch (start us, length us, event | category | flops | bytes accessed | tf_op | source)
XLA Modules:
  0.0 19.4 jit_solution(15437840122204900517)
XLA Ops:
  0.0 17.5 %level.1 = bf16[2,8,64,192]{3,2,1,0:T(8,128)(2,1)} custom-call(bf16[2,4,64,192]{3,2,1,0:T(8,128)(2,1)} %frames.1, bf16[2,4,64,192]{3,2,1,0:T(8,128)(2,1)} %cache.1, f32[1,192]{1,0:T(1,128)} %bitcast.7, bf16[27,192,192]{2,1,0:T(8,128)(2,1)} %bitcast.5, f32[1,192]{1,0:T(1,128)} %bitcast.8, bf16[9,192,96]{2,1,0:T(8,128)(2,1)} %bitcast.6, f32[1,96]{1,0:T(1,128)} %bitcast.9), custom_call_target="tpu_custom_call" | custom-call | tf_op jit(solution)/shard_map/level/pallas_call | solution.py:335
  17.5 1.9 %copy.9 = bf16[2,8,64,192]{3,2,1,0:T(8,128)(2,1)} copy(bf16[2,8,64,192]{3,2,1,0:T(8,128)(2,1)} %level.1) | data formatting | bytes 786432
